TPU v7x, 32 devices: a whole 2x2x4 slice. The times are simulated.
32 devices in a mesh: dp: 8 (over y, x, core), mp: 4 (over z).
Axes of the slice: x: 2, y: 2, z: 4, core: 2. Of those that a mesh axis runs over, the one named last changes fastest.
Arguments:
- activations: bfloat16 [16384, 1024], P('dp'), may hold values from -6 to 6
- cotangent: bfloat16 [16384, 1024], P('dp'), may hold values from -6 to 6
- level_table: bfloat16 [1024, 1024], P('dp'), may hold values from -6 to 6
- true_frames: int32 [16], P('dp'), may hold values from 4 to 16
- group_pattern: int32 [16], P('dp'), may hold values from 0 to 3
- noise_levels: int32 [4, 16], replicated, may hold values from 1 to 1023
- context_flags: int32 [16, 16], P('dp'), may hold values 0 or 1
- owner_list: int32 [288], replicated, may hold values from 0 to 287, as said below
- masters: float32 [4, 288, 128, 128], P('mp', 'dp')
- moment_one: float32 [4, 288, 128, 128], P('mp', 'dp')
- moment_two: float32 [4, 288, 128, 128], P('mp', 'dp')
- basis_left: float32 [4, 288, 128, 128], P('mp', 'dp'), as said below
- basis_right: float32 [4, 288, 128, 128], P('mp', 'dp'), as said below
Outputs:
- block_output: bfloat16 [16384, 1024], P('dp')
- input_grad: float32 [16384, 1024], P('dp')
- table_grad: float32 [1024, 1024], P(('dp', 'mp'))
- new_masters: float32 [4, 288, 128, 128], P('mp', 'dp')
- new_moment_one: float32 [4, 288, 128, 128], P('mp', 'dp')
- new_moment_two: float32 [4, 288, 128, 128], P('mp', 'dp')
- new_weights: bfloat16 [4, 288, 128, 128], P('mp', 'dp')
Inputs may be any that keep to these rules, and one draw needn't show every extreme that they name: `owner_list`: each tile number appears once; position p belongs to the dp index p // 36. `basis_left`: every tile is an orthogonal matrix. `basis_right`: every tile is an orthogonal matrix.
All inputs are finite; a program needn't handle non-finite values. No bound on the sum of `context_flags` on one device may be relied on, other than what follows from the above.
Results may differ from a plain program's by a relative error of at most 0.02.
Values may be sent and summed in bfloat16 or wider, within the bound.
A program may use at most 256 MiB of HBM per device.

v0:
```python
import jax
import jax.numpy as jnp
from jax import lax
from jax.sharding import PartitionSpec as P

D = 1024
H = 16
HD = 64
FF = 4096
FRAMES = 16
FRAME_TOK = 64
LEVELS = 1024
PATTERNS = 4
TILE = 128
HIGHEST = lax.Precision.HIGHEST
EPS_NORM = 1e-06
BETA_ONE = 0.5
BETA_TWO = 0.75
EPS_ADAM = 1e-08
DECAY = 0.01


def tile_layout(model_width, heads, head_dim, hidden, groups, tile_size):
    local_width = heads // groups * head_dim
    shapes = [
        (model_width, 3 * local_width),
        (local_width, model_width),
        (model_width, hidden // groups),
        (hidden // groups, model_width),
        (model_width, 6 * model_width // groups),
    ]
    counts = [height // tile_size * (breadth // tile_size) for height, breadth in shapes]
    return (shapes, counts)


def unpack(tile_stack, shapes, counts, tile_size):
    matrices = []
    offset = 0
    for (height, breadth), amount in zip(shapes, counts):
        stacked = tile_stack[offset : offset + amount].reshape(
            height // tile_size, breadth // tile_size, tile_size, tile_size
        )
        matrices.append(stacked.transpose(0, 2, 1, 3).reshape(height, breadth))
        offset = offset + amount
    return matrices


def pack(matrices, tile_size):
    stacked = []
    for matrix in matrices:
        height, breadth = matrix.shape
        stacked.append(
            matrix.reshape(height // tile_size, tile_size, breadth // tile_size, tile_size)
            .transpose(0, 2, 1, 3)
            .reshape(-1, tile_size, tile_size)
        )
    return jnp.concatenate(stacked, axis=0)


def kind_rates(tile_ids, counts):
    scales = [
        0.35 * D ** (-0.5),
        1.5 * (H * HD) ** (-0.5),
        0.5 * D ** (-0.5),
        0.5 * FF ** (-0.5),
        0.5 * D ** (-0.5),
    ]
    tile_rates = jnp.full(tile_ids.shape, scales[0], jnp.float32)
    boundary = 0
    for category in range(1, 5):
        boundary = boundary + counts[category - 1]
        tile_rates = jnp.where(tile_ids >= boundary, jnp.float32(scales[category]), tile_rates)
    return tile_rates


def layer_norm(stream):
    centered = stream - jnp.mean(stream, axis=-1, keepdims=True)
    inverse_std = lax.rsqrt(jnp.mean(centered * centered, axis=-1, keepdims=True) + EPS_NORM)
    return (centered * inverse_std, inverse_std)


def norm_back(grad_normed, normed, inverse_std):
    centered_grad = grad_normed - jnp.mean(grad_normed, axis=-1, keepdims=True)
    return inverse_std * (
        centered_grad - normed * jnp.mean(grad_normed * normed, axis=-1, keepdims=True)
    )


def gelu_tanh(values):
    return jax.nn.gelu(values, approximate=True)


def gelu_back(values, incoming):
    _, pullback = jax.vjp(gelu_tanh, values)
    return pullback(incoming)[0]


def contract_rows(left_side, right_side):
    return lax.dot_general(
        left_side, right_side, (((0,), (0,)), ((), ())), preferred_element_type=jnp.float32
    )


def contract_cols(left_side, right_side):
    return lax.dot_general(
        left_side, right_side, (((1,), (1,)), ((), ())), preferred_element_type=jnp.float32
    )


def block_scores(queries, key_all, mask_rows, score_scale):
    scores = (
        jnp.einsum("cqhd,ckhd->chqk", queries, key_all, preferred_element_type=jnp.float32)
        * score_scale
    )
    return jnp.where(mask_rows[:, None], scores, -1e30)


def attend_block(queries, key_all, value_all, mask_rows, score_scale):
    scores = block_scores(queries, key_all, mask_rows, score_scale)
    row_peak = jnp.max(scores, axis=-1, keepdims=True)
    exp_scores = jnp.exp(scores - row_peak)
    row_total = jnp.sum(exp_scores, axis=-1, keepdims=True)
    soft_rows = (exp_scores / row_total).astype(jnp.bfloat16)
    attended = jnp.einsum(
        "chqk,ckhd->cqhd", soft_rows, value_all, preferred_element_type=jnp.float32
    )
    return (attended, row_peak + jnp.log(row_total))


def attend_back(queries, key_all, value_all, mask_rows, log_total, grad_rows, score_scale):
    scores = block_scores(queries, key_all, mask_rows, score_scale)
    soft_rows = jnp.exp(scores - log_total)
    grad_soft = jnp.einsum(
        "cqhd,ckhd->chqk", grad_rows, value_all, preferred_element_type=jnp.float32
    )
    row_delta = jnp.sum(soft_rows * grad_soft, axis=-1, keepdims=True)
    grad_scores = (soft_rows * (grad_soft - row_delta)).astype(jnp.bfloat16)
    grad_query = (
        jnp.einsum("chqk,ckhd->cqhd", grad_scores, key_all, preferred_element_type=jnp.float32)
        * score_scale
    )
    grad_key = (
        jnp.einsum("chqk,cqhd->ckhd", grad_scores, queries, preferred_element_type=jnp.float32)
        * score_scale
    )
    grad_value = jnp.einsum(
        "chqk,cqhd->ckhd",
        soft_rows.astype(jnp.bfloat16),
        grad_rows,
        preferred_element_type=jnp.float32,
    )
    return (grad_query, grad_key, grad_value)


def body(
    activations,
    cotangent,
    level_table,
    true_frames,
    group_pattern,
    noise_levels,
    context_flags,
    owner_list,
    masters,
    moment_one,
    moment_two,
    basis_left,
    basis_right,
):
    groups = lax.axis_size("mp")
    member = lax.axis_index("mp")
    owner_rank = lax.axis_index("dp")
    shapes, counts = tile_layout(D, H, HD, FF, groups, TILE)
    slot_count = masters.shape[1]
    clip_count = true_frames.shape[0]
    frame_rows = clip_count * FRAMES
    tok_rows = activations.shape[0]
    clip_len = FRAMES * FRAME_TOK
    score_scale = HD ** (-0.5)
    inverse = jnp.argsort(owner_list)
    gathered, level_rows = (
        lax.all_gather(masters.astype(jnp.bfloat16), "dp", axis=1, tiled=True),
        lax.all_gather(level_table, "dp", axis=0, tiled=True),
    )
    w_qkv, w_out, w_up, w_down, w_mod = unpack(
        jnp.take(gathered[0], inverse, axis=0), shapes, counts, TILE
    )
    local_width = w_out.shape[0]
    heads_here = local_width // HD
    frame_index = jnp.arange(FRAMES, dtype=jnp.int32)
    valid_frame = frame_index[None, :] < true_frames[:, None]
    flagged = context_flags == 1
    in_context = flagged & valid_frame
    visible = valid_frame[:, None, :] & (
        jnp.logical_not(in_context)[:, :, None] | in_context[:, None, :]
    )
    pattern_hot = (group_pattern[:, None] == jnp.arange(PATTERNS, dtype=jnp.int32)[None, :]).astype(
        jnp.int32
    )
    pattern_levels = jnp.sum(pattern_hot[:, :, None] * noise_levels[None, :, :], axis=1)
    levels = jnp.where(flagged, 0, pattern_levels)
    level_hot = (
        levels.reshape(-1)[:, None] == jnp.arange(LEVELS, dtype=jnp.int32)[None, :]
    ).astype(jnp.bfloat16)
    embedded = jnp.dot(level_hot, level_rows, preferred_element_type=jnp.float32).astype(
        jnp.bfloat16
    )
    mod_part = jnp.dot(embedded, w_mod, preferred_element_type=jnp.float32)
    mod_all = lax.all_gather(mod_part, "mp", axis=1, tiled=True)
    modulation = (
        mod_all.reshape(frame_rows, groups, 6, D // groups)
        .transpose(0, 2, 1, 3)
        .reshape(frame_rows, 6, D)
    )
    token_mask = jnp.repeat(jnp.repeat(visible, FRAME_TOK, axis=1), FRAME_TOK, axis=2)
    stream = activations.astype(jnp.float32).reshape(frame_rows, FRAME_TOK, D)
    normed_one, inverse_one = layer_norm(stream)
    hidden_one = (
        (normed_one * (1.0 + modulation[:, 1, None, :]) + modulation[:, 0, None, :])
        .astype(jnp.bfloat16)
        .reshape(tok_rows, D)
    )
    qkv_rows = jnp.dot(hidden_one, w_qkv, preferred_element_type=jnp.float32).astype(jnp.bfloat16)
    queries = qkv_rows[:, :local_width].reshape(clip_count, clip_len, heads_here, HD)
    key_rows = qkv_rows[:, local_width : 2 * local_width].reshape(
        clip_count, clip_len, heads_here, HD
    )
    value_rows = qkv_rows[:, 2 * local_width :].reshape(clip_count, clip_len, heads_here, HD)
    block_rows = min(512, clip_len)
    block_total = clip_len // block_rows
    attended_parts = []
    log_parts = []
    for block_id in range(block_total):
        first_row = block_id * block_rows
        attended_blk, log_blk = attend_block(
            queries[:, first_row : first_row + block_rows],
            key_rows,
            value_rows,
            token_mask[:, first_row : first_row + block_rows],
            score_scale,
        )
        attended_parts.append(attended_blk)
        log_parts.append(log_blk)
    attended = (
        jnp.concatenate(attended_parts, axis=1).astype(jnp.bfloat16).reshape(tok_rows, local_width)
    )
    branch = (
        lax.psum(
            jnp.dot(attended, w_out, preferred_element_type=jnp.float32).astype(jnp.bfloat16), "mp"
        )
        .astype(jnp.float32)
        .reshape(frame_rows, FRAME_TOK, D)
    )
    middle = stream + modulation[:, 2, None, :] * branch
    normed_two, inverse_two = layer_norm(middle)
    hidden_two = (
        (normed_two * (1.0 + modulation[:, 4, None, :]) + modulation[:, 3, None, :])
        .astype(jnp.bfloat16)
        .reshape(tok_rows, D)
    )
    pre_act = jnp.dot(hidden_two, w_up, preferred_element_type=jnp.float32)
    activated = gelu_tanh(pre_act).astype(jnp.bfloat16)
    feed_out = (
        lax.psum(
            jnp.dot(activated, w_down, preferred_element_type=jnp.float32).astype(jnp.bfloat16),
            "mp",
        )
        .astype(jnp.float32)
        .reshape(frame_rows, FRAME_TOK, D)
    )
    result = middle + modulation[:, 5, None, :] * feed_out
    block_output = result.reshape(tok_rows, D).astype(jnp.bfloat16)
    regathered = lax.all_gather(masters.astype(jnp.bfloat16), "dp", axis=1, tiled=True)
    back_qkv, back_out, back_up, back_down, back_mod = unpack(
        jnp.take(regathered[0], inverse, axis=0), shapes, counts, TILE
    )
    grad_out = cotangent.astype(jnp.float32).reshape(frame_rows, FRAME_TOK, D)
    grad_feed = (modulation[:, 5, None, :] * grad_out).astype(jnp.bfloat16).reshape(tok_rows, D)
    grad_down = contract_rows(activated, grad_feed)
    grad_act = contract_cols(grad_feed, back_down).astype(jnp.bfloat16)
    grad_pre = gelu_back(pre_act, grad_act.astype(jnp.float32)).astype(jnp.bfloat16)
    grad_up = contract_rows(hidden_two, grad_pre)
    grad_gate_two = jnp.sum(grad_out * feed_out, axis=1)
    grad_hidden_two = (
        lax.psum(contract_cols(grad_pre, back_up).astype(jnp.bfloat16), "mp")
        .astype(jnp.float32)
        .reshape(frame_rows, FRAME_TOK, D)
    )
    grad_shift_two = jnp.sum(grad_hidden_two, axis=1)
    grad_scale_two = jnp.sum(grad_hidden_two * normed_two, axis=1)
    grad_middle = grad_out + norm_back(
        grad_hidden_two * (1.0 + modulation[:, 4, None, :]), normed_two, inverse_two
    )
    grad_gate_one = jnp.sum(grad_middle * branch, axis=1)
    grad_branch = (
        (modulation[:, 2, None, :] * grad_middle).astype(jnp.bfloat16).reshape(tok_rows, D)
    )
    grad_out_proj = contract_rows(attended, grad_branch)
    grad_attended = (
        contract_cols(grad_branch, back_out)
        .astype(jnp.bfloat16)
        .reshape(clip_count, clip_len, heads_here, HD)
    )
    query_parts = []
    grad_key = jnp.zeros((clip_count, clip_len, heads_here, HD), jnp.float32)
    grad_value = jnp.zeros((clip_count, clip_len, heads_here, HD), jnp.float32)
    for block_id in range(block_total):
        first_row = block_id * block_rows
        grad_query_blk, grad_key_blk, grad_value_blk = attend_back(
            queries[:, first_row : first_row + block_rows],
            key_rows,
            value_rows,
            token_mask[:, first_row : first_row + block_rows],
            log_parts[block_id],
            grad_attended[:, first_row : first_row + block_rows],
            score_scale,
        )
        query_parts.append(grad_query_blk)
        grad_key = grad_key + grad_key_blk
        grad_value = grad_value + grad_value_blk
    grad_query = jnp.concatenate(query_parts, axis=1)
    grad_qkv = jnp.concatenate(
        [
            grad_query.astype(jnp.bfloat16).reshape(tok_rows, local_width),
            grad_key.astype(jnp.bfloat16).reshape(tok_rows, local_width),
            grad_value.astype(jnp.bfloat16).reshape(tok_rows, local_width),
        ],
        axis=1,
    )
    grad_w_qkv = contract_rows(hidden_one, grad_qkv)
    grad_hidden_one = (
        lax.psum(contract_cols(grad_qkv, back_qkv).astype(jnp.bfloat16), "mp")
        .astype(jnp.float32)
        .reshape(frame_rows, FRAME_TOK, D)
    )
    grad_shift_one = jnp.sum(grad_hidden_one, axis=1)
    grad_scale_one = jnp.sum(grad_hidden_one * normed_one, axis=1)
    input_grad = (
        grad_middle
        + norm_back(grad_hidden_one * (1.0 + modulation[:, 1, None, :]), normed_one, inverse_one)
    ).reshape(tok_rows, D)
    grad_mod = jnp.stack(
        [
            grad_shift_one,
            grad_scale_one,
            grad_gate_one,
            grad_shift_two,
            grad_scale_two,
            grad_gate_two,
        ],
        axis=1,
    )
    grad_mod_own = lax.dynamic_index_in_dim(
        grad_mod.reshape(frame_rows, 6, groups, D // groups), member, axis=2, keepdims=False
    )
    grad_mod_own = grad_mod_own.reshape(frame_rows, 6 * D // groups).astype(jnp.bfloat16)
    grad_w_mod = contract_rows(embedded, grad_mod_own)
    grad_embedded = contract_cols(grad_mod_own, back_mod)
    table_term = lax.dot_general(
        level_hot.astype(jnp.float32),
        grad_embedded,
        (((0,), (0,)), ((), ())),
        precision=HIGHEST,
        preferred_element_type=jnp.float32,
    )
    table_grad = lax.psum_scatter(table_term, ("dp", "mp"), scatter_dimension=0, tiled=True)
    packed = pack([grad_w_qkv, grad_out_proj, grad_up, grad_down, grad_w_mod], TILE)
    owned = jnp.take(packed, owner_list, axis=0)
    reduced = lax.psum_scatter(
        owned[None].astype(jnp.bfloat16), "dp", scatter_dimension=1, tiled=True
    ).astype(jnp.float32)[0]
    tile_ids = lax.dynamic_slice_in_dim(owner_list, owner_rank * slot_count, slot_count)
    rotated = jnp.einsum("pji,pjk->pik", basis_left[0], reduced, precision=HIGHEST)
    rotated = jnp.einsum("pik,pkl->pil", rotated, basis_right[0], precision=HIGHEST)
    new_one = BETA_ONE * moment_one[0] + (1.0 - BETA_ONE) * rotated
    new_two = BETA_TWO * moment_two[0] + (1.0 - BETA_TWO) * rotated * rotated
    direction = new_one / (jnp.sqrt(new_two) + EPS_ADAM)
    turned = jnp.einsum("pij,pjk->pik", basis_left[0], direction, precision=HIGHEST)
    turned = jnp.einsum("pik,plk->pil", turned, basis_right[0], precision=HIGHEST)
    tile_rates = kind_rates(tile_ids, counts)
    new_masters = masters[0] - tile_rates[:, None, None] * (turned + DECAY * masters[0])
    return (
        block_output,
        input_grad,
        table_grad,
        new_masters[None],
        new_one[None],
        new_two[None],
        new_masters[None].astype(jnp.bfloat16),
    )


def solution(mesh):
    in_specs = (
        P("dp", None),
        P("dp", None),
        P("dp", None),
        P("dp"),
        P("dp"),
        P(),
        P("dp", None),
        P(),
        P("mp", "dp", None, None),
        P("mp", "dp", None, None),
        P("mp", "dp", None, None),
        P("mp", "dp", None, None),
        P("mp", "dp", None, None),
    )
    out_specs = (
        P("dp", None),
        P("dp", None),
        P(("dp", "mp"), None),
        P("mp", "dp", None, None),
        P("mp", "dp", None, None),
        P("mp", "dp", None, None),
        P("mp", "dp", None, None),
    )
    return jax.shard_map(body, mesh=mesh, in_specs=in_specs, out_specs=out_specs, check_vma=False)
```

profile of v0, /device:TPU:0, one launch (start us, length us, event | category | flops | bytes accessed | tf_op | source)
XLA Modules:
  0.0 1286.3 jit_solution(2902918120802603525)
XLA Ops:
  32.7 8.9 all-gather.3.cloned.1.call-done
  43.8 59.1 %all-gather.5.cloned.1.call-done = bf16[1,288,128,128]{3,2,0,1:T(8,128)(2,1)} async-done(((bf16[1,36,128,128]{3,2,0,1:T(8,128)(2,1)}), bf16[1,288,128,128]{3,2,0,1:T(8,128)(2,1)}) %all-gather.5.cloned.1.call-update) | async-done | bytes 9437200 | tf_op jit(solution)/shard_map/all_gather | solution.py:182
  102.8 14.0 %gather_fusion.1 = bf16[288,128,128]{2,1,0:T(8,128)(2,1)} fusion(bf16[288,128,128]{2,1,0:T(8,128)(2,1)} %bitcast.414, s32[1024]{0:T(1024)S(1)} %pad_clamp_fusion.1), kind=kCustom, calls=%fused_computation.clone | custom fusion | bytes 18875520 | tf_op jit(solution)/shard_map/jit(_take)/gather | solution.py:186
  116.8 8.2 broadcast_select_fusion
  143.5 20.2 %all_gather.12 = f32[32,6144]{1,0:T(8,128)} all-gather(f32[32,1536]{1,0:T(8,128)S(1)} %fusion.68), channel_id=1, replica_groups=mesh['dp'=8,'mp'=4] {'mp'}, dimensions={1}, use_global_device_ids=true | all-gather | bytes 983040 | tf_op jit(solution)/shard_map/all_gather | solution.py:209
  253.9 137.4 %all-reduce.5.cloned.1.call-done = bf16[2048,1024]{1,0:T(8,128)(2,1)} async-done(((bf16[2048,1024]{1,0:T(8,128)(2,1)}), bf16[2048,1024]{1,0:T(8,128)(2,1)}) %all-reduce.5.cloned.1.call-update) | async-done | bytes 4194320 | tf_op jit(solution)/shard_map/psum | solution.py:248
  401.8 14.3 %fusion.40 = (bf16[1024,2048]{1,0:T(8,128)(2,1)}, bf16[1024,2048]{1,0:T(8,128)(2,1)}, f32[2048,1024]{0,1:T(8,128)S(1)}) fusion(bf16[2048,1024]{0,1:T(8,128)(2,1)} %convolution_convert_fusion.2, bf16[2048,1024]{1,0:T(8,128)(2,1)S(1)} %fusion.35, bf16[128,8,8,128]{3,2,1,0:T(8,128)(2,1)S(1)} %bitcast.439), kind=kOutput, calls=%fused_computation.70 | convolution fusion | flops 4343201792 | bytes 27262976 | tf_op jit(solution)/shard_map/dot_general | solution.py:261
  419.5 12.9 %fusion.63 = bf16[2048,1024]{1,0:T(8,128)(2,1)} fusion(f32[2048,1024]{0,1:T(8,128)S(1)} %get-tuple-element.58, bf16[2048,1024]{0,1:T(8,128)(2,1)} %convolution_convert_fusion.2, bf16[128,8,8,128]{3,2,1,0:T(8,128)(2,1)S(1)} %bitcast.440), kind=kOutput, calls=%fused_computation.107 | convolution fusion | flops 4341104640 | bytes 18874368 | tf_op jit(solution)/shard_map/dot_general | solution.py:105
  433.8 12.7 fusion.62
  446.5 140.1 %all-reduce.7.cloned.1.call-done = bf16[2048,1024]{1,0:T(8,128)(2,1)} async-done(((bf16[2048,1024]{1,0:T(8,128)(2,1)}), bf16[2048,1024]{1,0:T(8,128)(2,1)}) %all-reduce.7.cloned.1.call-update) | async-done | bytes 4194320 | tf_op jit(solution)/shard_map/psum | solution.py:285
  586.6 7.9 fusion.54
  594.9 8.3 fusion.28
  616.5 14.2 %multiply_reduce_fusion.1 = (f32[2,4,512]{2,1,0:T(4,128)S(1)}, f32[2,4,512,1024]{3,2,1,0:T(8,128)}) fusion(f32[2,4,512,1024]{3,2,1,0:T(8,128)} %copy-done.5, f32[2,4,512]{2,1,0:T(4,128)} %bitcast.454, bf16[2,512,4,64]{1,3,2,0:T(8,128)(2,1)} %copy.253, bf16[2,1024,4,64]{1,3,2,0:T(8,128)(2,1)} %copy.198), kind=kOutput, calls=%fused_computation.8 | convolution fusion | flops 549449728 | bytes 35160064 | tf_op jit(solution)/shard_map/cqhd,ckhd->chqk/dot_general | solution.py:133
  633.4 10.3 multiply_convert_fusion.1
  643.8 7.3 fusion.114
  655.3 7.6 fusion.36
  663.0 13.7 %multiply_reduce_fusion = (f32[2,4,512]{2,1,0:T(4,128)S(1)}, f32[2,4,512,1024]{3,2,1,0:T(8,128)}) fusion(f32[2,4,512,1024]{3,2,1,0:T(8,128)} %copy-done.4, f32[2,4,512]{2,1,0:T(4,128)S(1)} %bitcast.452, bf16[2,512,4,64]{1,3,2,0:T(8,128)(2,1)S(1)} %copy-done.30, bf16[2,1024,4,64]{1,3,2,0:T(8,128)(2,1)S(1)} %copy-done.21), kind=kOutput, calls=%fused_computation.5 | convolution fusion | flops 549449728 | bytes 35160064 | tf_op jit(solution)/shard_map/cqhd,ckhd->chqk/dot_general | solution.py:133
  676.6 9.2 fusion.106
  688.3 10.7 multiply_convert_fusion
  719.5 6.9 copy.240
  726.4 6.5 copy.237
  734.2 6.5 copy.239
  740.7 8.7 fusion.161
  756.6 6.5 copy.238
  776.0 230.9 %all-reduce.9.cloned.1.call-done = (bf16[2048,1024]{1,0:T(8,128)(2,1)}, bf16[2048,1024]{1,0:T(8,128)(2,1)}) async-done(((bf16[2048,1024]{1,0:T(8,128)(2,1)}, bf16[2048,1024]{1,0:T(8,128)(2,1)}), (bf16[2048,1024]{1,0:T(8,128)(2,1)}, bf16[2048,1024]{1,0:T(8,128)(2,1)})) %all-reduce.9.cloned.1.call-update) | async-done | bytes 8388624 | tf_op jit(solution)/shard_map/psum | solution.py:264
  1006.8 17.0 %fusion.49 = (bf16[32,1024]{1,0:T(8,128)(2,1)S(1)}, bf16[32,1024]{1,0:T(8,128)(2,1)S(1)}, bf16[32,1024]{1,0:T(8,128)(2,1)S(1)}, bf16[32,1024]{1,0:T(8,128)(2,1)S...) fusion(bf16[2048,1024]{1,0:T(8,128)(2,1)} %all-reduce.7.cloned.1.call-done, ...), kind=kLoop, calls=%fused_computation.83 | loop fusion | flops 58523648 | bytes 25870336 | tf_op jit(solution)/shard_map/reduce_sum | solution.py:290
  1027.8 14.0 %gather_fusion = bf16[288,128,128]{2,1,0:T(8,128)(2,1)} fusion(bf16[288,128,128]{2,1,0:T(8,128)(2,1)} %constant_dynamic-update-slice_fusion.9, s32[1024]{0:T(1024)S(1)} %copy-done.78), kind=kCustom, calls=%fused_computation.1 | custom fusion | bytes 18875520 | tf_op jit(solution)/shard_map/jit(_take)/gather | solution.py:368
  1041.8 9.3 fusion
  1058.6 8.1 fusion.43
  1067.1 12.4 fusion.46
  1079.5 47.6 %reduce-scatter.5.cloned.1.call-done = bf16[1,36,128,128]{3,2,1,0:T(8,128)(2,1)} async-done(((bf16[1,288,128,128]{3,2,1,0:T(8,128)(2,1)}), bf16[1,36,128,128]{3,2,1,0:T(8,128)(2,1)}) %reduce-scatter.5.cloned.1.call-update) | async-done | bytes 1179664 | tf_op jit(solution)/shard_map/reduce_scatter | solution.py:369
  1149.4 129.7 %reduce-scatter.3.cloned.1.call-done = f32[32,1024]{1,0:T(8,128)} async-done(((f32[1024,1024]{1,0:T(8,128)}), f32[32,1024]{1,0:T(8,128)}) %reduce-scatter.3.cloned.1.call-update) | async-done | bytes 131088 | tf_op jit(solution)/shard_map/reduce_scatter | solution.py:366
  (333 shorter events, 249.6 us)
Async XLA Ops:
  7.2 1119.9 %copy-start = (f32[1,36,128,128]{3,2,1,0:T(8,128)S(1)}, f32[1,36,128,128]{3,2,1,0:T(8,128)}, u32[]{:S(2)}) copy-start(f32[1,36,128,128]{3,2,1,0:T(8,128)} %param.26) | copy-start | bytes 7077892
  7.2 15.9 %copy-start.76 = (s32[288]{0:T(512)S(1)}, s32[288]{0:T(512)}, u32[]{:S(2)}) copy-start(s32[288]{0:T(512)} %param.22) | copy-start | bytes 3460
  7.2 34.5 %all-gather.3.cloned.1.call-start = ((), (), s32[]{:S(2)}) async-start(), calls=%async_computation.2 | async-start | bytes 2359296 | tf_op jit(solution)/shard_map/all_gather | solution.py:183
  7.9 94.9 %all-gather.5.cloned.1.call-start = ((), (), s32[]{:S(2)}) async-start(), calls=%async_computation.3 | async-start | bytes 10616832 | tf_op jit(solution)/shard_map/all_gather | solution.py:182
  10.9 380.4 %all-reduce.5.cloned.1.call-start = ((), (), s32[]{:S(2)}) async-start(), calls=%async_computation.4 | async-start | bytes 8388608 | tf_op jit(solution)/shard_map/psum | solution.py:248
  13.2 28.5 %copy-start.79 = (s32[32]{0:T(128)}, s32[32]{0:T(128)S(1)}, u32[]{:S(2)}) copy-start(s32[32]{0:T(128)S(1)} %eq.43) | copy-start | bytes 388
  29.7 139.1 %copy-start.56 = (f32[2048]{0:T(1024)}, f32[2048]{0:T(1024)S(1)}, u32[]{:S(2)}) copy-start(f32[2048]{0:T(1024)S(1)} %broadcast_multiply_fusion.5) | copy-start | bytes 24580
  32.7 136.1 %copy-start.62 = (f32[2048]{0:T(1024)}, f32[2048]{0:T(1024)S(1)}, u32[]{:S(2)}) copy-start(f32[2048]{0:T(1024)S(1)} %add_rsqrt_fusion.1) | copy-start | bytes 24580
  43.7 96.9 %copy-start.52 = (bf16[32,1024]{1,0:T(8,128)(2,1)}, bf16[32,1024]{1,0:T(8,128)(2,1)S(1)}, u32[]{:S(2)}) copy-start(bf16[32,1024]{1,0:T(8,128)(2,1)S(1)} %convolution_convert_fusion.5) | copy-start | bytes 196612
  182.1 35.7 %copy-start.13 = (bf16[2,1024,4,64]{1,3,2,0:T(8,128)(2,1)}, bf16[2,1024,4,64]{1,3,2,0:T(8,128)(2,1)S(1)}, u32[]{:S(2)}) copy-start(bf16[2,1024,4,64]{1,3,2,0:T(8,128)(2,1)S(1)} %copy.197) | copy-start | bytes 3145732
  237.3 349.3 %all-reduce.7.cloned.1.call-start = ((), (), s32[]{:S(2)}) async-start(), calls=%async_computation.5 | async-start | bytes 8388608 | tf_op jit(solution)/shard_map/psum | solution.py:285
  401.8 14.3 %copy-start.18 = (bf16[2048,1024]{1,0:T(8,128)(2,1)}, bf16[2048,1024]{1,0:T(8,128)(2,1)S(1)}, u32[]{:S(2)}) copy-start(bf16[2048,1024]{1,0:T(8,128)(2,1)S(1)} %fusion.35) | copy-start | bytes 12582916
  419.5 13.6 %copy-start.67 = (f32[2,4,512]{2,1,0:T(4,128)S(1)}, f32[2,4,512]{2,1,0:T(4,128)}, u32[]{:S(2)}) copy-start(f32[2,4,512]{2,1,0:T(4,128)} %copy-done.66) | copy-start | bytes 49156
  432.5 574.3 %all-reduce.9.cloned.1.call-start = ((), (), s32[]{:S(2)}) async-start(), calls=%async_computation.8 | async-start | bytes 16777216 | tf_op jit(solution)/shard_map/psum | solution.py:264
  616.5 14.2 %slice-start.4 = ((s8[16777216]{0:T(1024)(128)(4,1)}), s8[4194304]{0:T(1024)(128)(4,1)S(1)}, s32[]{:S(2)}) async-start(s8[16777216]{0:T(1024)(128)(4,1)} %bitcast.403), calls=%async_computation.13 | async-start | bytes 8388608
  616.5 14.2 %slice-start.5 = ((s8[16777216]{0:T(1024)(128)(4,1)}), s8[4194304]{0:T(1024)(128)(4,1)S(1)}, s32[]{:S(2)}) async-start(s8[16777216]{0:T(1024)(128)(4,1)} %bitcast.403), calls=%async_computation.14 | async-start | bytes 8388608
  616.5 15.7 %slice-start.6 = ((s8[16777216]{0:T(1024)(128)(4,1)}), s8[4194304]{0:T(1024)(128)(4,1)S(1)}, s32[]{:S(2)}) async-start(s8[16777216]{0:T(1024)(128)(4,1)} %bitcast.403), calls=%async_computation.15 | async-start | bytes 8388608
  616.5 16.9 %slice-start.7 = ((s8[16777216]{0:T(1024)(128)(4,1)}), s8[4194304]{0:T(1024)(128)(4,1)S(1)}, s32[]{:S(2)}) async-start(s8[16777216]{0:T(1024)(128)(4,1)} %bitcast.403), calls=%async_computation.16 | async-start | bytes 8388608
  616.5 16.9 %copy-start.59 = (f32[1,8,512]{2,1,0:T(8,128)S(1)}, f32[1,8,512]{2,1,0:T(8,128)}, u32[]{:S(2)}) copy-start(f32[1,8,512]{2,1,0:T(8,128)} %log_add_fusion.1) | copy-start | bytes 49156
  662.9 13.7 %copy-start.60 = (f32[1,8,512]{2,1,0:T(8,128)S(1)}, f32[1,8,512]{2,1,0:T(8,128)}, u32[]{:S(2)}) copy-start(f32[1,8,512]{2,1,0:T(8,128)} %log_add_fusion.1) | copy-start | bytes 49156
  662.9 25.3 %slice-start = ((s8[16777216]{0:T(1024)(128)(4,1)}), s8[4194304]{0:T(1024)(128)(4,1)S(1)}, s32[]{:S(2)}) async-start(s8[16777216]{0:T(1024)(128)(4,1)} %bitcast.401), calls=%async_computation.9 | async-start | bytes 8388608
  662.9 25.3 %slice-start.1 = ((s8[16777216]{0:T(1024)(128)(4,1)}), s8[4194304]{0:T(1024)(128)(4,1)S(1)}, s32[]{:S(2)}) async-start(s8[16777216]{0:T(1024)(128)(4,1)} %bitcast.401), calls=%async_computation.10 | async-start | bytes 8388608
  663.0 25.3 %slice-start.2 = ((s8[16777216]{0:T(1024)(128)(4,1)}), s8[4194304]{0:T(1024)(128)(4,1)S(1)}, s32[]{:S(2)}) async-start(s8[16777216]{0:T(1024)(128)(4,1)} %bitcast.401), calls=%async_computation.11 | async-start | bytes 8388608
  688.3 16.9 %copy-start.15 = (f32[2,4,64,1024]{3,2,1,0:T(8,128)S(1)}, f32[2,4,64,1024]{3,2,1,0:T(8,128)}, u32[]{:S(2)}) copy-start(f32[2,4,64,1024]{3,2,1,0:T(8,128)} %fusion.157) | copy-start | bytes 6291460
  716.8 410.2 %reduce-scatter.5.cloned.1.call-start = ((), (), s32[]{:S(2)}) async-start(), calls=%async_computation.7 | async-start | bytes 10616832 | tf_op jit(solution)/shard_map/reduce_scatter | solution.py:369
  770.8 236.0 %copy-start.37 = (f32[32,1024]{1,0:T(8,128)S(1)}, f32[32,1024]{1,0:T(8,128)}, u32[]{:S(2)}) copy-start(f32[32,1024]{1,0:T(8,128)} %get-tuple-element.43) | copy-start | bytes 393220
  770.8 236.0 %copy-start.72 = (f32[32,64]{1,0:T(8,128)S(1)}, f32[32,64]{1,0:T(8,128)}, u32[]{:S(2)}) copy-start(f32[32,64]{1,0:T(8,128)} %rsqrt.27) | copy-start | bytes 24580
  770.8 236.0 %copy-start.73 = (f32[32,64]{1,0:T(8,128)S(1)}, f32[32,64]{1,0:T(8,128)}, u32[]{:S(2)}) copy-start(f32[32,64]{1,0:T(8,128)} %div.65) | copy-start | bytes 24580
  1006.8 17.8 %copy-start.61 = (bf16[4,8,8,128]{3,2,1,0:T(8,128)(2,1)S(1)}, bf16[4,8,8,128]{3,2,1,0:T(8,128)(2,1)}, u32[]{:S(2)}) copy-start(bf16[4,8,8,128]{3,2,1,0:T(8,128)(2,1)} %copy.266) | copy-start | bytes 196612
  1027.8 14.0 %copy-start.81 = (pred[288]{0:T(512)(128)(4,1)S(1)}, pred[288]{0:T(512)(128)(4,1)}, u32[]{:S(2)}) copy-start(pred[288]{0:T(512)(128)(4,1)} %compare_and_fusion.1) | copy-start | bytes 868
  1051.1 228.0 %reduce-scatter.3.cloned.1.call-start = ((), (), s32[]{:S(2)}) async-start(), calls=%async_computation.6 | async-start | bytes 4325376 | tf_op jit(solution)/shard_map/reduce_scatter | solution.py:366
  1053.7 13.0 %copy-start.51 = (f32[32,1024]{1,0:T(8,128)S(1)}, f32[32,1024]{1,0:T(8,128)}, u32[]{:S(2)}) copy-start(f32[32,1024]{1,0:T(8,128)} %get-tuple-element.45) | copy-start | bytes 393220
  (68 other events, 398.3 us)
Sparse Core Ops, SparseCore 0:
  9.9 31.7 all-gather.2
  44.1 58.6 all-gather.4
  237.4 153.8 all-reduce.4
  432.6 153.9 all-reduce.6
  717.0 289.8 all-reduce.8
  1051.2 75.7 reduce-scatter.4
  1129.9 149.1 reduce-scatter.2
where the time goes:
time: 1300 us; the launch traced here: 1290 us
  waiting for transfers between devices  754 us (58%)
  matrix products  191 us (15%)
  local copies, waits for them, and re-layouts  168 us (13%)
  other arithmetic  137 us (11%)
  blocking collectives  20.2 us (2%)
  between operations  15.8 us (1%)
    psum x1, waiting for transfers between devices, body(): lax.psum(jnp.dot(activated, w_down, preferred_element_type=jnp.float32).a...  231 us
    psum x1, waiting for transfers between devices, body(): lax.psum(contract_cols(grad_pre, back_up).astype(jnp.bfloat16), 'mp')  140 us
    psum x1, waiting for transfers between devices, body(): lax.psum(jnp.dot(attended, w_out, preferred_element_type=jnp.float32).ast...  137 us
    reduce_scatter x1, waiting for transfers between devices, body(): lax.psum_scatter(table_term, ('dp', 'mp'), scatter_dimension=0, tiled=True)  130 us
    all_gather x1, waiting for transfers between devices, body(): lax.all_gather(masters.astype(jnp.bfloat16), 'dp', axis=1, tiled=True)  59.1 us
    reduce_scatter x1, waiting for transfers between devices, body(): lax.psum_scatter(owned[None].astype(jnp.bfloat16), 'dp', scatter_dimensio...  47.6 us
    unnamed x205, local copies, waits for them, and re-layouts  36.9 us
    dot_general x5, matrix products, contract_cols(): lax.dot_general(left_side, right_side, (((1,), (1,)), ((), ())), preferre...  29.2 us
  transfers between devices with their start and end apart: 7, of which 7 were waited for; matrix products, arithmetic and copies ran while one was open for 13% of the time, Pallas kernels for 0%

commit v1 on v0

--- a/solution.py
+++ b/solution.py
@@ -18,6 +18,27 @@
 BETA_TWO = 0.75
 EPS_ADAM = 1e-08
 DECAY = 0.01
+
+
+def gather_around(x, axis, dim):
+    peers, position, span = (lax.axis_size(axis), lax.axis_index(axis), x.shape[dim])
+    forward = [(i, (i + 1) % peers) for i in range(peers)]
+    downward = [(i, (i - 1) % peers) for i in range(peers)]
+    out = jnp.zeros((*x.shape[:dim], peers * span, *x.shape[dim + 1 :]), x.dtype)
+    out = lax.dynamic_update_slice_in_dim(out, x, position * span, axis=dim)
+    from_left = from_right = x
+    middle = peers // 2
+    for turn in range(1, middle + 1):
+        from_left = lax.ppermute(from_left, axis, forward)
+        out = lax.dynamic_update_slice_in_dim(
+            out, from_left, (position - turn) % peers * span, axis=dim
+        )
+        if turn < peers - middle:
+            from_right = lax.ppermute(from_right, axis, downward)
+            out = lax.dynamic_update_slice_in_dim(
+                out, from_right, (position + turn) % peers * span, axis=dim
+            )
+    return out
 
 
 def tile_layout(model_width, heads, head_dim, hidden, groups, tile_size):
@@ -179,7 +200,7 @@
     score_scale = HD ** (-0.5)
     inverse = jnp.argsort(owner_list)
     gathered, level_rows = (
-        lax.all_gather(masters.astype(jnp.bfloat16), "dp", axis=1, tiled=True),
+        gather_around(masters.astype(jnp.bfloat16), "dp", 1),
         lax.all_gather(level_table, "dp", axis=0, tiled=True),
     )
     w_qkv, w_out, w_up, w_down, w_mod = unpack(

time: 1300 us -> 1370 us (1.054)
  local copies, waits for them, and re-layouts: 168 us -> 224 us
    ppermute x0 -> x7, waiting for transfers between devices: none -> 101 us  [the longest x4 88 us: gather_around(): from_left = lax.ppermute(from_left, axis, forward)]
    all_gather x1, waiting for transfers between devices: 59.1 us -> 0.01 us  [body(): lax.all_gather(masters.astype(jnp.bfloat16), 'dp', axis=1, tiled=True)]
    transpose x0 -> x5, local copies, waits for them, and re-layouts: none -> 14.5 us  [unpack(): matrices.append(stacked.transpose(0, 2, 1, 3).reshape(height, breadth))]
    gather x0 -> x1, local copies, waits for them, and re-layouts: none -> 14.1 us  [body(): jnp.take(regathered[0], inverse, axis=0)]
    unnamed x205 -> x221, local copies, waits for them, and re-layouts: 36.9 us -> 40.7 us
  transfers between devices with their start and end apart: 7 -> 14, of which waited for: 7 -> 10; matrix products, arithmetic and copies ran while one was open for 13% -> 16% of each run, Pallas kernels for 0% -> 0%
where the time goes in v1:
time: 1370 us; the launch traced here: 1360 us
  waiting for transfers between devices  767 us (56%)
  local copies, waits for them, and re-layouts  224 us (16%)
  matrix products  191 us (14%)
  other arithmetic  135 us (10%)
  blocking collectives  18.9 us (1%)
  between operations  15.8 us (1%)
    psum x1, waiting for transfers between devices, body(): lax.psum(jnp.dot(activated, w_down, preferred_element_type=jnp.float32).a...  231 us
    psum x1, waiting for transfers between devices, body(): lax.psum(jnp.dot(attended, w_out, preferred_element_type=jnp.float32).ast...  133 us
    psum x1, waiting for transfers between devices, body(): lax.psum(contract_cols(grad_pre, back_up).astype(jnp.bfloat16), 'mp')  130 us
    reduce_scatter x1, waiting for transfers between devices, body(): lax.psum_scatter(table_term, ('dp', 'mp'), scatter_dimension=0, tiled=True)  129 us
    ppermute x4, waiting for transfers between devices, gather_around(): from_left = lax.ppermute(from_left, axis, forward)  88 us
    unnamed x221, local copies, waits for them, and re-layouts  40.7 us
    reduce_scatter x1, waiting for transfers between devices, body(): lax.psum_scatter(owned[None].astype(jnp.bfloat16), 'dp', scatter_dimensio...  40.4 us
    dot_general x5, matrix products, contract_cols(): lax.dot_general(left_side, right_side, (((1,), (1,)), ((), ())), preferre...  28.8 us
  transfers between devices with their start and end apart: 14, of which 10 were waited for; matrix products, arithmetic and copies ran while one was open for 16% of the time, Pallas kernels for 0%

profile of v1, /device:TPU:0, one launch (start us, length us, event | category | flops | bytes accessed | tf_op | source)
XLA Modules:
  0.0 1360.4 jit_solution(6008438301689442595)
XLA Ops:
  22.4 33.2 %collective-permute-done = bf16[1,36,128,128]{3,2,0,1:T(8,128)(2,1)} collective-permute-done((bf16[1,36,128,128]{3,2,0,1:T(8,128)(2,1)}, bf16[1,36,128,128]{3,2,0,1:T(8,128)(2,1)}, u32[]{:S(2)}, u32[]{:S(2)}) %collective-permute-start) | collective-permute-done | bytes 1179680 | tf_op jit(solution)/shard_map/ppermute | solution.py:32
  73.1 18.1 %collective-permute-done.2 = bf16[1,36,128,128]{3,2,0,1:T(8,128)(2,1)} collective-permute-done((bf16[1,36,128,128]{3,2,0,1:T(8,128)(2,1)}, bf16[1,36,128,128]{3,2,0,1:T(8,128)(2,1)}, u32[]{:S(2)}, u32[]{:S(2)}) %collective-permute-start.2) | collective-permute-done | bytes 1179680 | tf_op jit(solution)/shard_map/ppermute | solution.py:32
  94.3 13.3 collective-permute-done.3
  115.3 27.8 %collective-permute-done.4 = bf16[1,36,128,128]{3,2,0,1:T(8,128)(2,1)S(1)} collective-permute-done((bf16[1,36,128,128]{3,2,0,1:T(8,128)(2,1)}, bf16[1,36,128,128]{3,2,0,1:T(8,128)(2,1)S(1)}, u32[]{:S(2)}, u32[]{:S(2)}) %collective-permute-start.4) | collective-permute-done | bytes 1179680 | tf_op jit(solution)/shard_map/ppermute | solution.py:32
  152.1 8.9 collective-permute-done.6
  163.5 14.1 %gather_fusion.1 = bf16[288,128,128]{2,1,0:T(8,128)(2,1)} fusion(bf16[288,128,128]{2,1,0:T(8,128)(2,1)} %bitcast_dynamic-update-slice_fusion, s32[1024]{0:T(1024)} %pad_clamp_fusion.1), kind=kCustom, calls=%fused_computation.clone | custom fusion | bytes 18875520 | tf_op jit(solution)/shard_map/jit(_take)/gather | solution.py:207
  177.6 14.1 %gather_fusion.2 = bf16[288,128,128]{2,1,0:T(8,128)(2,1)} fusion(bf16[288,128,128]{2,1,0:T(8,128)(2,1)} %bitcast.464, s32[1024]{0:T(1024)S(1)} %copy-done.81), kind=kCustom, calls=%fused_computation.1.clone | custom fusion | bytes 18875520 | tf_op jit(solution)/shard_map/jit(_take)/gather | solution.py:296
  191.7 12.0 broadcast_select_fusion
  221.4 18.9 %all_gather.10 = f32[32,6144]{1,0:T(8,128)} all-gather(f32[32,1536]{1,0:T(8,128)S(1)} %fusion.69), channel_id=1, replica_groups=mesh['dp'=8,'mp'=4] {'mp'}, dimensions={1}, use_global_device_ids=true | all-gather | bytes 983040 | tf_op jit(solution)/shard_map/all_gather | solution.py:230
  335.1 132.9 %all-reduce.5.cloned.1.call-done = bf16[2048,1024]{1,0:T(8,128)(2,1)} async-done(((bf16[2048,1024]{1,0:T(8,128)(2,1)}), bf16[2048,1024]{1,0:T(8,128)(2,1)}) %all-reduce.5.cloned.1.call-update) | async-done | bytes 4194320 | tf_op jit(solution)/shard_map/psum | solution.py:269
  478.6 15.2 %fusion.40 = (bf16[1024,2048]{1,0:T(8,128)(2,1)}, bf16[1024,2048]{1,0:T(8,128)(2,1)}, f32[2048,1024]{0,1:T(8,128)S(1)}) fusion(bf16[2048,1024]{0,1:T(8,128)(2,1)} %convolution_convert_fusion.2, bf16[2048,1024]{1,0:T(8,128)(2,1)S(1)} %fusion.35, bf16[128,8,8,128]{3,2,1,0:T(8,128)(2,1)S(1)} %bitcast.491), kind=kOutput, calls=%fused_computation.72 | convolution fusion | flops 4343201792 | bytes 27262976 | tf_op jit(solution)/shard_map/dot_general | solution.py:282
  497.2 12.7 fusion.63
  522.1 11.5 fusion.62
  533.6 130.4 %all-reduce.7.cloned.1.call-done = bf16[2048,1024]{1,0:T(8,128)(2,1)} async-done(((bf16[2048,1024]{1,0:T(8,128)(2,1)}), bf16[2048,1024]{1,0:T(8,128)(2,1)}) %all-reduce.7.cloned.1.call-update) | async-done | bytes 4194320 | tf_op jit(solution)/shard_map/psum | solution.py:306
  664.0 6.5 fusion.54
  672.3 8.4 fusion.28
  690.8 14.2 %multiply_reduce_fusion.1 = (f32[2,4,512]{2,1,0:T(4,128)S(1)}, f32[2,4,512,1024]{3,2,1,0:T(8,128)}) fusion(f32[2,4,512,1024]{3,2,1,0:T(8,128)} %copy-done.5, f32[2,4,512]{2,1,0:T(4,128)} %bitcast.510, bf16[2,512,4,64]{1,3,2,0:T(8,128)(2,1)} %copy.273, bf16[2,1024,4,64]{1,3,2,0:T(8,128)(2,1)} %copy.213), kind=kOutput, calls=%fused_computation.9 | convolution fusion | flops 549449728 | bytes 35160064 | tf_op jit(solution)/shard_map/cqhd,ckhd->chqk/dot_general | solution.py:154
  707.8 10.1 multiply_convert_fusion.1
  717.9 7.3 fusion.114
  729.5 7.6 fusion.36
  737.1 13.8 %multiply_reduce_fusion = (f32[2,4,512]{2,1,0:T(4,128)S(1)}, f32[2,4,512,1024]{3,2,1,0:T(8,128)}) fusion(f32[2,4,512,1024]{3,2,1,0:T(8,128)} %copy-done.4, f32[2,4,512]{2,1,0:T(4,128)S(1)} %bitcast.508, bf16[2,512,4,64]{1,3,2,0:T(8,128)(2,1)S(1)} %copy-done.32, bf16[2,1024,4,64]{1,3,2,0:T(8,128)(2,1)S(1)} %copy-done.22), kind=kOutput, calls=%fused_computation.6 | convolution fusion | flops 549449728 | bytes 35160064 | tf_op jit(solution)/shard_map/cqhd,ckhd->chqk/dot_general | solution.py:154
  750.9 9.1 fusion.106
  762.4 10.5 multiply_convert_fusion
  793.8 6.5 copy.260
  814.6 8.7 fusion.162
  849.8 231.4 %all-reduce.9.cloned.1.call-done = (bf16[2048,1024]{1,0:T(8,128)(2,1)}, bf16[2048,1024]{1,0:T(8,128)(2,1)}) async-done(((bf16[2048,1024]{1,0:T(8,128)(2,1)}, bf16[2048,1024]{1,0:T(8,128)(2,1)}), (bf16[2048,1024]{1,0:T(8,128)(2,1)}, bf16[2048,1024]{1,0:T(8,128)(2,1)})) %all-reduce.9.cloned.1.call-update) | async-done | bytes 8388624 | tf_op jit(solution)/shard_map/psum | solution.py:285
  1081.2 17.0 %fusion.49 = (bf16[32,1024]{1,0:T(8,128)(2,1)S(1)}, bf16[32,1024]{1,0:T(8,128)(2,1)S(1)}, bf16[32,1024]{1,0:T(8,128)(2,1)S(1)}, bf16[32,1024]{1,0:T(8,128)(2,1)S...) fusion(bf16[2048,1024]{1,0:T(8,128)(2,1)} %all-reduce.7.cloned.1.call-done, ...), kind=kLoop, calls=%fused_computation.85 | loop fusion | flops 58523648 | bytes 25870336 | tf_op jit(solution)/shard_map/reduce_sum | solution.py:311
  1102.2 14.0 %gather_fusion = bf16[288,128,128]{2,1,0:T(8,128)(2,1)} fusion(bf16[288,128,128]{2,1,0:T(8,128)(2,1)} %constant_dynamic-update-slice_fusion.9, s32[1024]{0:T(1024)S(1)} %copy-done.82), kind=kCustom, calls=%fused_computation.2 | custom fusion | bytes 18875520 | tf_op jit(solution)/shard_map/jit(_take)/gather | solution.py:389
  1116.2 9.2 fusion
  1148.7 12.3 fusion.46
  1161.0 40.4 %reduce-scatter.5.cloned.1.call-done = bf16[1,36,128,128]{3,2,1,0:T(8,128)(2,1)} async-done(((bf16[1,288,128,128]{3,2,1,0:T(8,128)(2,1)}), bf16[1,36,128,128]{3,2,1,0:T(8,128)(2,1)}) %reduce-scatter.5.cloned.1.call-update) | async-done | bytes 1179664 | tf_op jit(solution)/shard_map/reduce_scatter | solution.py:390
  1223.7 129.5 %reduce-scatter.3.cloned.1.call-done = f32[32,1024]{1,0:T(8,128)} async-done(((f32[1024,1024]{1,0:T(8,128)}), f32[32,1024]{1,0:T(8,128)}) %reduce-scatter.3.cloned.1.call-update) | async-done | bytes 131088 | tf_op jit(solution)/shard_map/reduce_scatter | solution.py:387
  (380 shorter events, 325.1 us)
Async XLA Ops:
  7.2 1194.2 %copy-start = (f32[1,36,128,128]{3,2,1,0:T(8,128)S(1)}, f32[1,36,128,128]{3,2,1,0:T(8,128)}, u32[]{:S(2)}) copy-start(f32[1,36,128,128]{3,2,1,0:T(8,128)} %param.26) | copy-start | bytes 7077892
  7.2 142.1 %all-gather.3.cloned.1.call-start = ((), (), s32[]{:S(2)}) async-start(), calls=%async_computation.2 | async-start | bytes 2359296 | tf_op jit(solution)/shard_map/all_gather | solution.py:204
  8.0 169.6 %all-gather.5.cloned.1.call-start = ((), (), s32[]{:S(2)}) async-start(), calls=%async_computation.4 | async-start | bytes 10616832 | tf_op jit(solution)/shard_map/all_gather | solution.py:294
  14.0 48.8 %copy-start.79 = (s32[288]{0:T(512)S(1)}, s32[288]{0:T(512)}, u32[]{:S(2)}) copy-start(s32[288]{0:T(512)} %param.22) | copy-start | bytes 3460
  16.1 451.9 %all-reduce.5.cloned.1.call-start = ((), (), s32[]{:S(2)}) async-start(), calls=%async_computation.3 | async-start | bytes 8388608 | tf_op jit(solution)/shard_map/psum | solution.py:269
  16.1 51.5 %collective-permute-start.1 = (bf16[1,36,128,128]{3,2,0,1:T(8,128)(2,1)}, bf16[1,36,128,128]{3,2,0,1:T(8,128)(2,1)}, u32[]{:S(2)}, u32[]{:S(2)}) collective-permute-start(bf16[1,36,128,128]{3,2,0,1:T(8,128)(2,1)} %get-tuple-element.27), channel_id=1, source_target_pairs={{0,28},{4,0},{8,4},{12,8},{16,12},{20,16},{24,20},{28,24},{1,29},{... | collective-permute-start | bytes 3538952 | tf_op jit(solution)/shard_map/ppermute | solution.py:37
  19.5 36.1 %collective-permute-start = (bf16[1,36,128,128]{3,2,0,1:T(8,128)(2,1)}, bf16[1,36,128,128]{3,2,0,1:T(8,128)(2,1)}, u32[]{:S(2)}, u32[]{:S(2)}) collective-permute-start(bf16[1,36,128,128]{3,2,0,1:T(8,128)(2,1)} %get-tuple-element.27), channel_id=1, source_target_pairs={{0,4},{4,8},{8,12},{12,16},{16,20},{20,24},{24,28},{28,0},{1,5},{5... | collective-permute-start | bytes 3538952 | tf_op jit(solution)/shard_map/ppermute | solution.py:32
  55.6 35.7 %collective-permute-start.2 = (bf16[1,36,128,128]{3,2,0,1:T(8,128)(2,1)}, bf16[1,36,128,128]{3,2,0,1:T(8,128)(2,1)}, u32[]{:S(2)}, u32[]{:S(2)}) collective-permute-start(bf16[1,36,128,128]{3,2,0,1:T(8,128)(2,1)} %collective-permute-done), channel_id=1, source_target_pairs={{0,4},{4,8},{8,12},{12,16},{16,20},{20,24},{24,28},{28,0},{1,5},{5... | collective-permute-start | bytes 3538952 | tf_op jit(solution)/shard_map/ppermute | solution.py:32
  67.7 39.9 %collective-permute-start.3 = (bf16[1,36,128,128]{3,2,0,1:T(8,128)(2,1)}, bf16[1,36,128,128]{3,2,0,1:T(8,128)(2,1)S(1)}, u32[]{:S(2)}, u32[]{:S(2)}) collective-permute-start(bf16[1,36,128,128]{3,2,0,1:T(8,128)(2,1)} %collective-permute-done.1), channel_id=1, source_target_pairs={{0,28},{4,0},{8,4},{12,8},{16,12},{20,16},{24,20},{28,24},{1,29},{... | collective-permute-start | bytes 3538952 | tf_op jit(solution)/shard_map/ppermute | solution.py:37
  73.1 172.2 %copy-start.59 = (f32[2048]{0:T(1024)}, f32[2048]{0:T(1024)S(1)}, u32[]{:S(2)}) copy-start(f32[2048]{0:T(1024)S(1)} %broadcast_multiply_fusion.5) | copy-start | bytes 24580
  91.3 51.8 %collective-permute-start.4 = (bf16[1,36,128,128]{3,2,0,1:T(8,128)(2,1)}, bf16[1,36,128,128]{3,2,0,1:T(8,128)(2,1)S(1)}, u32[]{:S(2)}, u32[]{:S(2)}) collective-permute-start(bf16[1,36,128,128]{3,2,0,1:T(8,128)(2,1)} %collective-permute-done.2), channel_id=1, source_target_pairs={{0,4},{4,8},{8,12},{12,16},{16,20},{20,24},{24,28},{28,0},{1,5},{5... | collective-permute-start | bytes 3538952 | tf_op jit(solution)/shard_map/ppermute | solution.py:32
  94.3 151.0 %copy-start.65 = (f32[2048]{0:T(1024)}, f32[2048]{0:T(1024)S(1)}, u32[]{:S(2)}) copy-start(f32[2048]{0:T(1024)S(1)} %add_rsqrt_fusion.1) | copy-start | bytes 24580
  107.6 40.6 %collective-permute-start.5 = (bf16[1,36,128,128]{3,2,0,1:T(8,128)(2,1)S(1)}, bf16[1,36,128,128]{3,2,0,1:T(8,128)(2,1)S(1)}, u32[]{:S(2)}, u32[]{:S(2)}) collective-permute-start(bf16[1,36,128,128]{3,2,0,1:T(8,128)(2,1)S(1)} %collective-permute-done.3), channel_id=1, source_target_pairs={{0,28},{4,0},{8,4},{12,8},{16,12},{20,16},{24,20},{28,24},{1,29},{... | collective-permute-start | bytes 3538952 | tf_op jit(solution)/shard_map/ppermute | solution.py:37
  143.1 17.9 %collective-permute-start.6 = (bf16[1,36,128,128]{3,2,0,1:T(8,128)(2,1)S(1)}, bf16[1,36,128,128]{3,2,0,1:T(8,128)(2,1)}, u32[]{:S(2)}, u32[]{:S(2)}) collective-permute-start(bf16[1,36,128,128]{3,2,0,1:T(8,128)(2,1)S(1)} %collective-permute-done.4), channel_id=1, source_target_pairs={{0,4},{4,8},{8,12},{12,16},{16,20},{20,24},{24,28},{28,0},{1,5},{5... | collective-permute-start | bytes 3538952 | tf_op jit(solution)/shard_map/ppermute | solution.py:32
  258.6 35.7 %copy-start.14 = (bf16[2,1024,4,64]{1,3,2,0:T(8,128)(2,1)}, bf16[2,1024,4,64]{1,3,2,0:T(8,128)(2,1)S(1)}, u32[]{:S(2)}) copy-start(bf16[2,1024,4,64]{1,3,2,0:T(8,128)(2,1)S(1)} %copy.212) | copy-start | bytes 3145732
  313.7 350.4 %all-reduce.7.cloned.1.call-start = ((), (), s32[]{:S(2)}) async-start(), calls=%async_computation.5 | async-start | bytes 8388608 | tf_op jit(solution)/shard_map/psum | solution.py:306
  478.6 15.3 %copy-start.19 = (bf16[2048,1024]{1,0:T(8,128)(2,1)}, bf16[2048,1024]{1,0:T(8,128)(2,1)S(1)}, u32[]{:S(2)}) copy-start(bf16[2048,1024]{1,0:T(8,128)(2,1)S(1)} %fusion.35) | copy-start | bytes 12582916
  478.6 18.6 %copy-start.45 = (bf16[8,8,128,128]{3,1,2,0:T(8,128)(2,1)S(1)}, bf16[8,8,128,128]{3,1,2,0:T(8,128)(2,1)}, u32[]{:S(2)}) copy-start(bf16[8,8,128,128]{3,1,2,0:T(8,128)(2,1)} %copy.223) | copy-start | bytes 6291460
  509.9 571.3 %all-reduce.9.cloned.1.call-start = ((), (), s32[]{:S(2)}) async-start(), calls=%async_computation.8 | async-start | bytes 16777216 | tf_op jit(solution)/shard_map/psum | solution.py:285
  690.8 15.7 %slice-start.6 = ((s8[16777216]{0:T(1024)(128)(4,1)}), s8[4194304]{0:T(1024)(128)(4,1)S(1)}, s32[]{:S(2)}) async-start(s8[16777216]{0:T(1024)(128)(4,1)} %bitcast.454), calls=%async_computation.15 | async-start | bytes 8388608
  690.8 16.9 %slice-start.7 = ((s8[16777216]{0:T(1024)(128)(4,1)}), s8[4194304]{0:T(1024)(128)(4,1)S(1)}, s32[]{:S(2)}) async-start(s8[16777216]{0:T(1024)(128)(4,1)} %bitcast.454), calls=%async_computation.16 | async-start | bytes 8388608
  690.8 16.9 %copy-start.62 = (f32[1,8,512]{2,1,0:T(8,128)S(1)}, f32[1,8,512]{2,1,0:T(8,128)}, u32[]{:S(2)}) copy-start(f32[1,8,512]{2,1,0:T(8,128)} %log_add_fusion.1) | copy-start | bytes 49156
  737.1 25.3 %slice-start = ((s8[16777216]{0:T(1024)(128)(4,1)}), s8[4194304]{0:T(1024)(128)(4,1)S(1)}, s32[]{:S(2)}) async-start(s8[16777216]{0:T(1024)(128)(4,1)} %bitcast.452), calls=%async_computation.9 | async-start | bytes 8388608
  737.1 25.3 %slice-start.1 = ((s8[16777216]{0:T(1024)(128)(4,1)}), s8[4194304]{0:T(1024)(128)(4,1)S(1)}, s32[]{:S(2)}) async-start(s8[16777216]{0:T(1024)(128)(4,1)} %bitcast.452), calls=%async_computation.10 | async-start | bytes 8388608
  737.1 25.3 %slice-start.2 = ((s8[16777216]{0:T(1024)(128)(4,1)}), s8[4194304]{0:T(1024)(128)(4,1)S(1)}, s32[]{:S(2)}) async-start(s8[16777216]{0:T(1024)(128)(4,1)} %bitcast.452), calls=%async_computation.11 | async-start | bytes 8388608
  762.4 16.7 %copy-start.16 = (f32[2,4,64,1024]{3,2,1,0:T(8,128)S(1)}, f32[2,4,64,1024]{3,2,1,0:T(8,128)}, u32[]{:S(2)}) copy-start(f32[2,4,64,1024]{3,2,1,0:T(8,128)} %fusion.158) | copy-start | bytes 6291460
  791.2 410.2 %reduce-scatter.5.cloned.1.call-start = ((), (), s32[]{:S(2)}) async-start(), calls=%async_computation.7 | async-start | bytes 10616832 | tf_op jit(solution)/shard_map/reduce_scatter | solution.py:390
  844.7 236.5 %copy-start.39 = (f32[32,1024]{1,0:T(8,128)S(1)}, f32[32,1024]{1,0:T(8,128)}, u32[]{:S(2)}) copy-start(f32[32,1024]{1,0:T(8,128)} %get-tuple-element.47) | copy-start | bytes 393220
  844.7 236.5 %copy-start.75 = (f32[32,64]{1,0:T(8,128)S(1)}, f32[32,64]{1,0:T(8,128)}, u32[]{:S(2)}) copy-start(f32[32,64]{1,0:T(8,128)} %rsqrt.27) | copy-start | bytes 24580
  844.7 236.5 %copy-start.76 = (f32[32,64]{1,0:T(8,128)S(1)}, f32[32,64]{1,0:T(8,128)}, u32[]{:S(2)}) copy-start(f32[32,64]{1,0:T(8,128)} %div.65) | copy-start | bytes 24580
  1081.2 17.8 %copy-start.64 = (bf16[4,8,8,128]{3,2,1,0:T(8,128)(2,1)S(1)}, bf16[4,8,8,128]{3,2,1,0:T(8,128)(2,1)}, u32[]{:S(2)}) copy-start(bf16[4,8,8,128]{3,2,1,0:T(8,128)(2,1)} %copy.291) | copy-start | bytes 196612
  1125.4 227.8 %reduce-scatter.3.cloned.1.call-start = ((), (), s32[]{:S(2)}) async-start(), calls=%async_computation.6 | async-start | bytes 4325376 | tf_op jit(solution)/shard_map/reduce_scatter | solution.py:387
  (82 other events, 580.7 us)
Sparse Core Ops, SparseCore 0:
  9.9 38.9 all-gather.2
  51.4 90.7 all-gather.4
  313.8 154.1 all-reduce.4
  510.0 153.9 all-reduce.6
  791.3 289.8 all-reduce.8
  1125.5 75.7 reduce-scatter.4
  1204.2 148.9 reduce-scatter.2
